TPU v7x, 256 devices: a whole 4x4x8 slice. The times are simulated.
256 devices in a mesh: ctx: 32 (over z_lo, y, x), head: 8 (over z_hi, core).
Axes of the slice: x: 4, y: 4, z: 8 (z_hi: 4, z_lo: 2; z = z_hi * 2 + z_lo), core: 2. Of those that a mesh axis runs over, the one named last changes fastest.
Arguments:
- queries: bfloat16 [8192, 5120], P('ctx', 'head'), may hold values from -800 to 800
- keys: bfloat16 [8192, 5120], P('ctx', 'head'), may hold values from -800 to 800
- values: bfloat16 [8192, 5120], P('ctx', 'head'), may hold values from -6 to 6
- q_gain: float32 [5120], P('head'), may hold values from 0.6 to 1.5
- k_gain: float32 [5120], P('head'), may hold values from 0.6 to 1.5
- ref_keys: bfloat16 [32768, 5120], P('ctx', 'head'), may hold values from -6 to 6
- ref_values: bfloat16 [32768, 5120], P('ctx', 'head'), may hold values from -6 to 6
- out_weight: bfloat16 [5120, 5120], P('head'), may hold values from -0.078125 to 0.078125
- partners: int32 [32, 2, 12], replicated, may hold values from 0 to 63, as said below
- owners: int32 [2], replicated, may hold values from 0 to 31, as said below
- labels: int32 [64], P('ctx'), may hold values from 0 to 1
Outputs:
- attended: bfloat16 [8192, 5120], P('ctx', 'head')
- mixed: bfloat16 [8192, 5120], P('ctx', 'head')
Inputs may be any that keep to these rules, and one draw needn't show every extreme that they name: `partners`: over both persons' lists of one context shard, the blocks of any one shard are named at most 1 times, and the blocks of some shard exactly 1 times. `owners`: the persons' identity shards differ, and one of them is the last shard.
All inputs are finite; a program needn't handle non-finite values.
Results may differ from a plain program's by a relative error of at most 0.018.
Values may be sent and summed in bfloat16 or wider, within the bound.
A program may use at most 128 MiB of HBM per device.

v0:
```python
import jax
import jax.numpy as jnp
from jax import lax
from jax.sharding import PartitionSpec as P

D = 5120
HD = 128
BLK = 128
epsilon = 1e-06


def spread(value, axis, source):
    kept = jnp.where(lax.axis_index(axis) == source, value, 0).astype(value.dtype)
    return lax.psum(kept, axis)


def normalize(features, scale_gain, square_total):
    factor = lax.rsqrt(square_total / D + epsilon)
    return (features * factor[:, None] * scale_gain[None, :]).astype(jnp.bfloat16)


def attend_block(query, own_keys, own_values, far_keys, far_values, bank_keys, bank_values):
    row_count, width = query.shape
    head_count = width // HD
    key_set = jnp.concatenate([own_keys, far_keys, bank_keys], axis=0)
    value_set = jnp.concatenate([own_values, far_values, bank_values], axis=0)
    query_heads = query.reshape(row_count, head_count, HD)
    key_heads = key_set.reshape(-1, head_count, HD)
    value_heads = value_set.reshape(-1, head_count, HD)
    scores = jnp.einsum(
        "qhd,khd->hqk", query_heads, key_heads, preferred_element_type=jnp.float32
    ) * HD ** (-0.5)
    row_peak = jnp.max(scores, axis=2, keepdims=True)
    exponent = jnp.exp(scores - row_peak)
    denominator = jnp.sum(exponent, axis=2)
    weights = exponent.astype(jnp.bfloat16)
    combined = jnp.einsum("hqk,khd->qhd", weights, value_heads, preferred_element_type=jnp.float32)
    return (combined / denominator.T[:, :, None]).reshape(row_count, width).astype(jnp.bfloat16)


def shards(
    queries,
    keys,
    values,
    q_gain,
    k_gain,
    ref_keys,
    ref_values,
    out_weight,
    partners,
    owners,
    labels,
):
    tokens, width = queries.shape
    blocks = tokens // BLK
    own_index = lax.axis_index("ctx")
    persons = partners.shape[1]
    q_float = queries.astype(jnp.float32)
    k_float = keys.astype(jnp.float32)
    q_total, k_total = lax.psum(
        (jnp.sum(q_float * q_float, axis=1), jnp.sum(k_float * k_float, axis=1)), "head"
    )
    q_norm = normalize(q_float, q_gain, q_total)
    k_norm = normalize(k_float, k_gain, k_total)
    query_blocks = q_norm.reshape(blocks, BLK, width)
    key_blocks = k_norm.reshape(blocks, BLK, width)
    value_blocks = values.reshape(blocks, BLK, width)
    wanted = partners[own_index].reshape(-1)
    whole_keys, whole_values = (
        lax.all_gather(k_norm, "ctx", axis=0, tiled=True),
        lax.all_gather(values, "ctx", axis=0, tiled=True),
    )
    far_keys = whole_keys.reshape(-1, BLK, width)[wanted]
    far_values = whole_values.reshape(-1, BLK, width)[wanted]
    far_keys = far_keys.reshape(persons, -1, width)
    far_values = far_values.reshape(persons, -1, width)
    local_bank = jnp.stack([ref_keys, ref_values])
    identities = []
    for person in range(persons):
        identities.append(spread(local_bank, "ctx", owners[person]))
    identity_stack = jnp.stack(identities)

    def one_block(position):
        person_label = labels[position]
        return attend_block(
            query_blocks[position],
            key_blocks[position],
            value_blocks[position],
            far_keys[person_label],
            far_values[person_label],
            identity_stack[person_label, 0],
            identity_stack[person_label, 1],
        )

    attended = lax.map(one_block, jnp.arange(blocks)).reshape(tokens, width)
    partial_out = jnp.dot(attended, out_weight, preferred_element_type=jnp.float32)
    mixed = lax.psum_scatter(
        partial_out.astype(jnp.bfloat16), "head", scatter_dimension=1, tiled=True
    )
    return (attended, mixed)


def solution(mesh):
    return jax.shard_map(
        shards,
        mesh=mesh,
        in_specs=(
            P("ctx", "head"),
            P("ctx", "head"),
            P("ctx", "head"),
            P("head"),
            P("head"),
            P("ctx", "head"),
            P("ctx", "head"),
            P("head", None),
            P(),
            P(),
            P("ctx"),
        ),
        out_specs=(P("ctx", "head"), P("ctx", "head")),
        check_vma=False,
    )
```

profile of v0, /device:TPU:28, one launch (start us, length us, event | category | flops | bytes accessed | tf_op | source)
XLA Modules:
  0.0 848.1 jit_solution(13434496772358359575)
XLA Ops:
  13.1 2.8 select_bitcast_fusion.1
  17.1 19.9 %all-reduce = (f32[256]{0:T(256)S(1)}, f32[256]{0:T(256)S(1)}) all-reduce(f32[256]{0:T(256)S(1)} %get-tuple-element.121, f32[256]{0:T(256)S(1)} %get-tuple-element.122), channel_id=1, replica_groups=mesh['ctx'=32,'head'=8] {'head'}, use_global_device_ids=true, to_apply=%region_1.0 | all-reduce | flops 512 | bytes 4096 | tf_op jit(solution)/shard_map/psum | solution.py:60
  40.0 308.8 %all-reduce.4.cloned.1.call-done = (bf16[1,2,1024,640]{2,3,1,0:T(8,128)(2,1)}, bf16[1,2,1024,640]{2,3,1,0:T(8,128)(2,1)}) async-done(((bf16[1,2,1024,640]{2,3,1,0:T(8,128)(2,1)}, bf16[1,2,1024,640]{2,3,1,0:T(8,128)(2,1)}), (bf16[1,2,1024,640]{2,3,1,0:T(8,128)(2,1)}, bf16[1,2,1024,640]{2,3,1,0:T(8,128)(2,1)})) %all-reduce.4.cloned.1.call-update) | async-done | bytes 5242896 | tf_op jit(solution)/shard_map/psum | solution.py:14
  348.8 5.3 pad_maximum_fusion
  354.1 169.4 %all-gather.5.cloned.1.call-done = bf16[8192,640]{1,0:T(8,128)(2,1)} async-done(((bf16[256,640]{1,0:T(8,128)(2,1)}), bf16[8192,640]{1,0:T(8,128)(2,1)}) %all-gather.5.cloned.1.call-update) | async-done | bytes 10485776 | tf_op jit(solution)/shard_map/all_gather | solution.py:70
  523.5 7.2 gather_fusion.1
  530.8 166.6 %all-gather.3.cloned.1.call-done = bf16[8192,640]{1,0:T(8,128)(2,1)} async-done(((bf16[256,640]{1,0:T(8,128)(2,1)}), bf16[8192,640]{1,0:T(8,128)(2,1)}) %all-gather.3.cloned.1.call-update) | async-done | bytes 10485776 | tf_op jit(solution)/shard_map/all_gather | solution.py:71
  697.4 7.2 gather_fusion
  704.7 75.3 %while.10 = (s32[]{:T(128)}, bf16[2,128,640]{2,1,0:T(8,128)(2,1)}, s32[2]{0:T(128)S(1)}, bf16[2,128,640]{2,1,0:T(8,128)(2,1)}, s32[2]{0:T(128)S(1)}, /*index=5*/...) while((s32[]{:T(128)}, bf16[2,128,640]{2,1,0:T(8,128)(2,1)}, ...), condition=%wide.region_9.10_spmd, body=%wide.region_6.9_spmd.sunk | while | flops 915372800 | bytes 109458328 | solution.py:95
  709.7 4.4 constant_dynamic-slice_fusion.14
  714.1 2.7 copy.74
  719.1 3.0 constant_dynamic-slice_fusion.13
  725.1 4.5 multiply_reduce_fusion.2
  732.7 2.4 copy.78
  736.2 5.1 fusion.55
  747.3 4.4 constant_dynamic-slice_fusion.14
  751.8 2.7 copy.74
  756.7 3.0 constant_dynamic-slice_fusion.13
  762.8 4.5 multiply_reduce_fusion.2
  770.3 2.4 copy.78
  773.8 5.1 fusion.55
  779.9 5.2 convolution_convert_fusion
  785.1 2.6 copy.54
  787.8 52.0 %reduce-scatter.4.cloned.1.call-done = bf16[640,256]{1,0:T(8,128)(2,1)} async-done(((bf16[5120,256]{1,0:T(8,128)(2,1)}), bf16[640,256]{1,0:T(8,128)(2,1)}) %reduce-scatter.4.cloned.1.call-update) | async-done | bytes 327696
  (88 shorter events, 33.6 us)
Async XLA Ops:
  7.2 31.6 %copy-start = (s32[32,2,12]{0,1,2:T(2,128)S(1)}, s32[32,2,12]{0,1,2:T(2,128)}, u32[]{:S(2)}) copy-start(s32[32,2,12]{0,1,2:T(2,128)} %param.21) | copy-start | bytes 9220
  7.2 341.6 %all-reduce.4.cloned.1.call-start = ((), (), s32[]{:S(2)}) async-start(), calls=%async_computation.4 | async-start | bytes 10485760 | tf_op jit(solution)/shard_map/psum | solution.py:14
  15.8 1.0 copy-start.6
  15.8 1.1 copy-start.7
  15.8 21.2 %copy-start.8 = (f32[640]{0:T(1024)S(1)}, f32[640]{0:T(1024)}, u32[]{:S(2)}) copy-start(f32[640]{0:T(1024)} %param.17) | copy-start | bytes 7684
  15.8 23.2 %copy-start.9 = (f32[640]{0:T(1024)S(1)}, f32[640]{0:T(1024)}, u32[]{:S(2)}) copy-start(f32[640]{0:T(1024)} %param.16) | copy-start | bytes 7684
  15.9 507.7 %all-gather.5.cloned.1.call-start = ((), (), s32[]{:S(2)}) async-start(), calls=%async_computation.2 | async-start | bytes 10813440 | tf_op jit(solution)/shard_map/all_gather | solution.py:70
  38.0 659.4 %all-gather.3.cloned.1.call-start = ((), (), s32[]{:S(2)}) async-start(), calls=%async_computation.1 | async-start | bytes 10813440 | tf_op jit(solution)/shard_map/all_gather | solution.py:71
  38.7 801.0 %reduce-scatter.4.cloned.1.call-start = ((), (), s32[]{:S(2)}) async-start(), calls=%async_computation.3 | async-start | bytes 2949120
  697.4 7.3 copy-start.12
  722.1 3.0 copy-start.4
  729.6 3.0 copy-start.3
  729.6 3.0 copy-start.2
  732.6 3.6 copy-start.5
  736.2 5.3 copy-start.10
  741.6 0.7 copy-start.11
  759.7 3.0 copy-start.4
  767.3 3.0 copy-start.3
  767.3 3.0 copy-start.2
  770.3 3.6 copy-start.5
  773.8 5.3 copy-start.10
  779.2 0.7 copy-start.11
  779.9 61.7 %copy-start.1 = (s32[32,2,12]{0,1,2:T(2,128)S(1)}, s32[32,2,12]{0,1,2:T(2,128)}, u32[]{:S(2)}) copy-start(s32[32,2,12]{0,1,2:T(2,128)} %param.21) | copy-start | bytes 9220
Sparse Core Ops, SparseCore 0:
  16.0 332.7 all-reduce.3
  350.5 172.9 all-gather.4
  525.3 172.0 all-gather.2
  787.9 51.7 reduce-scatter.3
where the time goes:
time: 849 us; the launch traced here: 848 us
  waiting for transfers between devices  698 us (82%)
  local copies, waits for them, and re-layouts  70.4 us (8%)
  matrix products  24.5 us (3%)
  blocking collectives  19.9 us (2%)
  between operations  15.2 us (2%)
  other arithmetic  12.6 us (1%)
    psum x1, waiting for transfers between devices, spread(): return lax.psum(kept, axis)  309 us
    all_gather x1, waiting for transfers between devices, shards(): lax.all_gather(k_norm, 'ctx', axis=0, tiled=True)  169 us
    all_gather x1, waiting for transfers between devices, shards(): lax.all_gather(values, 'ctx', axis=0, tiled=True)  167 us
    unnamed x5, waiting for transfers between devices  52.7 us
    psum x1, blocking collectives, shards(): lax.psum((jnp.sum(q_float * q_float, axis=1), jnp.sum(k_float * k_float,...  19.9 us
  transfers between devices with their start and end apart: 4, of which 4 were waited for; matrix products, arithmetic and copies ran while one was open for 2% of the time, Pallas kernels for 0%

commit v1 on v0

--- a/solution.py
+++ b/solution.py
@@ -67,7 +67,9 @@
     value_blocks = values.reshape(blocks, BLK, width)
     wanted = partners[own_index].reshape(-1)
     whole_keys, whole_values = (
-        lax.all_gather(k_norm, "ctx", axis=0, tiled=True),
+        jnp.concatenate(
+            lax.all_to_all(jnp.stack([k_norm] * lax.axis_size("ctx")), "ctx", 0, 0), axis=0
+        ),
         lax.all_gather(values, "ctx", axis=0, tiled=True),
     )
     far_keys = whole_keys.reshape(-1, BLK, width)[wanted]

time: 849 us -> 789 us (0.929)
  waiting for transfers between devices: 698 us -> 623 us
    all_gather x1 -> x0, waiting for transfers between devices: 169 us -> none  [shards(): lax.all_gather(k_norm, 'ctx', axis=0, tiled=True)]
    psum x1, waiting for transfers between devices: 309 us -> 409 us  [spread(): return lax.psum(kept, axis)]
    unnamed x5 -> x4, waiting for transfers between devices: 52.7 us -> 52 us
  transfers between devices with their start and end apart: 4 -> 4, of which waited for: 4 -> 3; matrix products, arithmetic and copies ran while one was open for 2% -> 3% of each run, Pallas kernels for 0% -> 0%
where the time goes in v1:
time: 789 us; the launch traced here: 787 us
  waiting for transfers between devices  623 us (79%)
  local copies, waits for them, and re-layouts  76.6 us (10%)
  matrix products  24.5 us (3%)
  blocking collectives  19.9 us (3%)
  between operations  15.1 us (2%)
  other arithmetic  12.6 us (2%)
  starting transfers between devices  8.32 us (1%)
    psum x1, waiting for transfers between devices, spread(): return lax.psum(kept, axis)  409 us
    all_gather x1, waiting for transfers between devices, shards(): lax.all_gather(values, 'ctx', axis=0, tiled=True)  162 us
    unnamed x4, waiting for transfers between devices  52 us
    psum x1, blocking collectives, shards(): lax.psum((jnp.sum(q_float * q_float, axis=1), jnp.sum(k_float * k_float,...  19.9 us
  transfers between devices with their start and end apart: 4, of which 3 were waited for; matrix products, arithmetic and copies ran while one was open for 3% of the time, Pallas kernels for 0%

profile of v1, /device:TPU:28, one launch (start us, length us, event | category | flops | bytes accessed | tf_op | source)
XLA Modules:
  0.0 787.3 jit_solution(3925018044978311522)
XLA Ops:
  13.1 2.7 select_bitcast_fusion.1
  17.0 19.9 %all-reduce = (f32[256]{0:T(256)S(1)}, f32[256]{0:T(256)S(1)}) all-reduce(f32[256]{0:T(256)S(1)} %fusion.35, f32[256]{0:T(256)S(1)} %fusion.38), channel_id=1, replica_groups=mesh['ctx'=32,'head'=8] {'head'}, use_global_device_ids=true, to_apply=%region_1.0 | all-reduce | flops 512 | bytes 4096 | tf_op jit(solution)/shard_map/psum | solution.py:60
  37.9 6.3 stack.20
  44.2 8.0 %all-to-all-start = ((bf16[32,256,640]{2,1,0:T(8,128)(2,1)}), bf16[32,256,640]{2,1,0:T(8,128)(2,1)}, u32[]{:S(2)}, u32[]{:S(2)}) async-start(bf16[32,256,640]{2,1,0:T(8,128)(2,1)} %stack.20), calls=%async_computation | async-start | bytes 20971520 | tf_op jit(solution)/shard_map/all_to_all | solution.py:71
  54.4 409.0 %all-reduce.4.cloned.1.call-done = (bf16[1,2,1024,640]{2,3,1,0:T(8,128)(2,1)}, bf16[1,2,1024,640]{2,3,1,0:T(8,128)(2,1)}) async-done(((bf16[1,2,1024,640]{2,3,1,0:T(8,128)(2,1)}, bf16[1,2,1024,640]{2,3,1,0:T(8,128)(2,1)}), (bf16[1,2,1024,640]{2,3,1,0:T(8,128)(2,1)}, bf16[1,2,1024,640]{2,3,1,0:T(8,128)(2,1)})) %all-reduce.4.cloned.1.call-update) | async-done | bytes 5242896 | tf_op jit(solution)/shard_map/psum | solution.py:14
  463.4 5.3 pad_maximum_fusion
  468.7 7.1 gather_fusion.1
  475.9 162.3 %all-gather.2.cloned.1.call-done = bf16[8192,640]{1,0:T(8,128)(2,1)} async-done(((bf16[256,640]{1,0:T(8,128)(2,1)}), bf16[8192,640]{1,0:T(8,128)(2,1)}) %all-gather.2.cloned.1.call-update) | async-done | bytes 10485776 | tf_op jit(solution)/shard_map/all_gather | solution.py:73
  638.2 7.2 gather_fusion
  645.4 74.4 %while.10 = (s32[]{:T(128)}, bf16[2,128,640]{2,1,0:T(8,128)(2,1)}, s32[2]{0:T(128)S(1)}, bf16[2,128,640]{2,1,0:T(8,128)(2,1)}, s32[2]{0:T(128)S(1)}, /*index=5*/...) while((s32[]{:T(128)}, bf16[2,128,640]{2,1,0:T(8,128)(2,1)}, ...), condition=%wide.region_9.10_spmd, body=%wide.region_6.9_spmd.sunk | while | flops 915372800 | bytes 109458328 | solution.py:97
  649.9 4.5 constant_dynamic-slice_fusion.14
  654.4 2.7 copy.74
  659.5 3.0 constant_dynamic-slice_fusion.13
  665.5 4.5 multiply_reduce_fusion.2
  673.0 2.4 copy.78
  676.5 5.1 fusion.55
  687.1 4.5 constant_dynamic-slice_fusion.14
  691.7 2.7 copy.74
  696.7 3.0 constant_dynamic-slice_fusion.13
  702.7 4.5 multiply_reduce_fusion.2
  713.7 5.1 fusion.55
  719.8 5.2 convolution_convert_fusion
  725.0 2.6 copy.54
  727.6 51.2 %reduce-scatter.4.cloned.1.call-done = bf16[640,256]{1,0:T(8,128)(2,1)} async-done(((bf16[5120,256]{1,0:T(8,128)(2,1)}), bf16[640,256]{1,0:T(8,128)(2,1)}) %reduce-scatter.4.cloned.1.call-update) | async-done | bytes 327696
  (88 shorter events, 36.1 us)
Async XLA Ops:
  7.2 46.1 %copy-start = (s32[32,2,12]{0,1,2:T(2,128)S(1)}, s32[32,2,12]{0,1,2:T(2,128)}, u32[]{:S(2)}) copy-start(s32[32,2,12]{0,1,2:T(2,128)} %param.21) | copy-start | bytes 9220
  7.2 456.3 %all-reduce.4.cloned.1.call-start = ((), (), s32[]{:S(2)}) async-start(), calls=%async_computation.4 | async-start | bytes 10485760 | tf_op jit(solution)/shard_map/psum | solution.py:14
  15.8 1.0 copy-start.7
  15.8 1.1 copy-start.6
  15.8 21.2 %copy-start.8 = (f32[640]{0:T(1024)S(1)}, f32[640]{0:T(1024)}, u32[]{:S(2)}) copy-start(f32[640]{0:T(1024)} %param.17) | copy-start | bytes 7684
  44.2 9.3 %copy-start.9 = (f32[640]{0:T(1024)S(1)}, f32[640]{0:T(1024)}, u32[]{:S(2)}) copy-start(f32[640]{0:T(1024)} %param.16) | copy-start | bytes 7684
  44.2 424.5 %all-to-all-start = ((bf16[32,256,640]{2,1,0:T(8,128)(2,1)}), bf16[32,256,640]{2,1,0:T(8,128)(2,1)}, u32[]{:S(2)}, u32[]{:S(2)}) async-start(bf16[32,256,640]{2,1,0:T(8,128)(2,1)} %stack.20), calls=%async_computation | async-start | bytes 20971520 | tf_op jit(solution)/shard_map/all_to_all | solution.py:71
  52.3 585.9 %all-gather.2.cloned.1.call-start = ((), (), s32[]{:S(2)}) async-start(), calls=%async_computation.2 | async-start | bytes 10813440 | tf_op jit(solution)/shard_map/all_gather | solution.py:73
  53.0 725.8 %reduce-scatter.4.cloned.1.call-start = ((), (), s32[]{:S(2)}) async-start(), calls=%async_computation.3 | async-start | bytes 2949120
  638.2 7.2 copy-start.12
  662.5 3.0 copy-start.4
  670.0 3.0 copy-start.3
  670.0 3.0 copy-start.2
  673.0 3.5 copy-start.5
  676.5 5.3 copy-start.10
  681.9 0.7 copy-start.11
  699.7 3.0 copy-start.4
  707.2 3.0 copy-start.3
  707.2 3.0 copy-start.2
  710.2 3.5 copy-start.5
  713.7 5.3 copy-start.10
  719.1 0.7 copy-start.11
  719.8 60.9 %copy-start.1 = (s32[32,2,12]{0,1,2:T(2,128)S(1)}, s32[32,2,12]{0,1,2:T(2,128)}, u32[]{:S(2)}) copy-start(s32[32,2,12]{0,1,2:T(2,128)} %param.21) | copy-start | bytes 9220
Sparse Core Ops, SparseCore 0:
  15.9 447.4 all-reduce.3
  465.2 172.9 all-gather.1
  727.8 51.0 reduce-scatter.3
